TPU v7x, 128 devices: a whole 4x4x4 slice. The times are simulated.
128 devices in a mesh: blk: 32 (over x, y, z_lo), segment: 4 (over z_hi, core).
Axes of the slice: x: 4, y: 4, z: 4 (z_hi: 2, z_lo: 2; z = z_hi * 2 + z_lo), core: 2. Of those that a mesh axis runs over, the one named last changes fastest.
Arguments:
- latent_queries: bfloat16 [2, 128, 2048], P(None, 'blk'), may hold values from -400 to 400
- latent_embed: bfloat16 [2, 128, 2048], P(None, 'blk'), may hold values from -6 to 6
- history_keys: bfloat16 [2, 32768, 2048], P(None, ('blk', 'segment')), may hold values from -6 to 6
- history_values: bfloat16 [2, 32768, 2048], P(None, ('blk', 'segment')), may hold values from -7 to 7
- latent_pos: int32 [2, 128], replicated, may hold values from 1 to 32768, as said below
- norm_gain: float32 [4, 2048], P('segment'), may hold values from 0.25 to 1.75
- w_qkv: bfloat16 [4, 2048, 3, 2048], P('segment', None, None, 'blk'), may hold values from -0.125 to 0.125
- w_out: bfloat16 [4, 2048, 2048], P('segment', 'blk'), may hold values from -0.125 to 0.125
Outputs:
- latents_out: float32 [2, 128, 2048], P(None, 'blk', 'segment')
Inputs may be any that keep to these rules, and one draw needn't show every extreme that they name: `latent_pos`: Non-decreasing along the latents of a micro-batch; latent i sees at least (i + 1) * 256 positions and the last latent sees all 32768.
All inputs are finite; a program needn't handle non-finite values.
Results may differ from a plain program's by a relative error of at most 0.0085.
Values may be sent and summed in bfloat16 or wider, within the bound.
A program may use at most 64 MiB of HBM per device.

v0:
```python
import jax
import jax.numpy as jnp
from jax import lax
from jax.sharding import PartitionSpec as P

HEADS = 16
epsilon = 1e-06
masked = -1e30


def from_partner(array, axis, distance):
    return lax.ppermute(array, axis, [(i, i ^ 1 << distance) for i in range(lax.axis_size(axis))])


def shifted(value, axis, steps):
    count = lax.axis_size(axis)
    first, last = (max(0, -steps), min(count, count - steps))
    return lax.ppermute(value, axis, [(source, source + steps) for source in range(first, last)])


def normalize(latent_state, gain_row):
    factor = lax.rsqrt(jnp.mean(latent_state * latent_state, axis=1, keepdims=True) + epsilon)
    return (latent_state * factor * gain_row).astype(jnp.bfloat16)


def attend_columns(mixed_qkv, head_size):
    lat_count = mixed_qkv.shape[0]
    columns = mixed_qkv.shape[1] // 3
    head_span = min(columns, head_size)
    head_groups = columns // head_span
    query_part = mixed_qkv[:, :columns].reshape(lat_count, head_groups, head_span)
    key_part = mixed_qkv[:, columns : 2 * columns].reshape(lat_count, head_groups, head_span)
    value_part = mixed_qkv[:, 2 * columns :].reshape(lat_count, head_groups, head_span)
    scores = jnp.einsum("ipd,jpd->pij", query_part, key_part, preferred_element_type=jnp.float32)
    scores = scores + from_partner(scores, "blk", 0)
    scores = scores * head_size ** (-0.5)
    row_ids = lax.broadcasted_iota(jnp.int32, (lat_count, lat_count), 0)
    col_ids = lax.broadcasted_iota(jnp.int32, (lat_count, lat_count), 1)
    scores = jnp.where((col_ids <= row_ids)[None], scores, masked)
    row_top = jnp.max(scores, axis=2, keepdims=True)
    weights = jnp.exp(scores - row_top)
    soft_weights = (weights / jnp.sum(weights, axis=2, keepdims=True)).astype(jnp.bfloat16)
    attended = jnp.einsum(
        "pij,jpd->ipd", soft_weights, value_part, preferred_element_type=jnp.float32
    )
    return attended.reshape(lat_count, columns).astype(jnp.bfloat16)


def layer_full(latent_state, gain_row, projection, output_rows, head_size):
    normed = normalize(latent_state, gain_row)
    mixed_qkv = jnp.dot(normed, projection, preferred_element_type=jnp.float32).astype(jnp.bfloat16)
    attended = attend_columns(mixed_qkv, head_size)
    update = jnp.dot(attended, output_rows, preferred_element_type=jnp.float32)
    return latent_state + lax.psum(update, "blk")


def on_device(
    latent_queries, latent_embed, history_keys, history_values, latent_pos, norm_gain, w_qkv, w_out
):
    segment_count = lax.axis_size("segment")
    blk_id = lax.axis_index("blk")
    segment_id = lax.axis_index("segment")
    micro_count = history_keys.shape[0]
    hist_rows = history_keys.shape[1]
    width = history_keys.shape[2]
    head_size = width // HEADS
    gathered = lax.all_gather(latent_queries, "blk", axis=1, tiled=True)
    lat_count = gathered.shape[1]
    first_key = (blk_id * segment_count + segment_id) * hist_rows
    key_ids = first_key + jnp.arange(hist_rows, dtype=jnp.int32)
    visible = (key_ids[None, None, :] < latent_pos[:, :, None])[:, None]
    query_heads = gathered.reshape(micro_count, lat_count, HEADS, head_size)
    key_heads = history_keys.reshape(micro_count, hist_rows, HEADS, head_size)
    value_heads = history_values.reshape(micro_count, hist_rows, HEADS, head_size)
    scores = jnp.einsum(
        "mqhd,mkhd->mhqk", query_heads, key_heads, preferred_element_type=jnp.float32
    ) * head_size ** (-0.5)
    scores = jnp.where(visible, scores, masked)
    highest = lax.pmax(jnp.max(scores, axis=3), ("blk", "segment"))
    weights = jnp.where(visible, jnp.exp(scores - highest[..., None]), 0.0)
    totals = jnp.transpose(jnp.sum(weights, axis=3), (0, 2, 1))
    partial_value = jnp.einsum(
        "mhqk,mkhd->mqhd",
        weights.astype(jnp.bfloat16),
        value_heads,
        preferred_element_type=jnp.float32,
    )
    partial_value = partial_value.reshape(micro_count, lat_count, width)
    summed, counted = (
        lax.psum_scatter(partial_value, "blk", scatter_dimension=1, tiled=True),
        lax.psum_scatter(totals, "blk", scatter_dimension=1, tiled=True),
    )
    summed, counted = lax.psum((summed, counted), "segment")
    rows_here = summed.shape[1]
    attended = (
        summed.reshape(micro_count, rows_here, HEADS, head_size) / counted[..., None]
    ).reshape(micro_count, rows_here, width)
    start_state = latent_embed.astype(jnp.float32) + attended
    gain_row = norm_gain[0]
    projection = w_qkv[0].reshape(width, -1)
    output_rows = w_out[0]
    tower_in = lax.all_gather(start_state, "blk", axis=1, tiled=True)
    rounds = micro_count + segment_count - 1
    last_segment = segment_count - 1
    incoming = jnp.zeros_like(tower_in[0])
    finished = []
    for round_index in range(rounds):
        if round_index < micro_count:
            incoming = jnp.where(segment_id == 0, tower_in[round_index], incoming)
        latent_state = layer_full(incoming, gain_row, projection, output_rows, head_size)
        if round_index >= last_segment:
            finished.append(jnp.where(segment_id == last_segment, latent_state, 0.0))
        if round_index + 1 < rounds:
            incoming = shifted(latent_state, "segment", 1)
    results = jnp.stack(finished)
    own_rows = latent_embed.shape[1]
    results = lax.dynamic_slice_in_dim(results, blk_id * own_rows, own_rows, 1)
    return lax.psum_scatter(results, "segment", scatter_dimension=2, tiled=True)


def solution(mesh):
    return jax.shard_map(
        on_device,
        mesh=mesh,
        in_specs=(
            P(None, "blk", None),
            P(None, "blk", None),
            P(None, ("blk", "segment"), None),
            P(None, ("blk", "segment"), None),
            P(),
            P("segment", None),
            P("segment", None, None, "blk"),
            P("segment", "blk", None),
        ),
        out_specs=P(None, "blk", "segment"),
        check_vma=False,
    )
```

profile of v0, /device:TPU:1, one launch (start us, length us, event | category | flops | bytes accessed | tf_op | source)
XLA Modules:
  0.0 2481.4 jit_solution(8695598158295302768)
XLA Ops:
  6.5 1.6 copy.17
  8.2 4.0 copy.28
  12.3 127.7 %all-gather.3.cloned.1.call-done = bf16[2,128,2048]{2,0,1:T(2,128)(2,1)} async-done(((bf16[2,4,2048]{2,0,1:T(2,128)(2,1)}), bf16[2,128,2048]{2,0,1:T(2,128)(2,1)}) %all-gather.3.cloned.1.call-update) | async-done | bytes 1048592 | tf_op jit(solution)/shard_map/all_gather | solution.py:67
  139.9 3.7 copy.18
  143.6 4.4 fusion
  148.0 87.3 %pmax.7 = f32[2,16,128]{2,1,0:T(8,128)S(1)} all-reduce(f32[2,16,128]{2,1,0:T(8,128)S(1)} %get-tuple-element.11), channel_id=1, replica_groups=mesh['blk'=32,'segment'=4] {'blk','segment'}, use_global_device_ids=true, to_apply=%region_1.2 | all-reduce | flops 4096 | bytes 32768 | tf_op jit(solution)/shard_map/pmax | solution.py:79
  235.3 5.4 fusion.3
  240.7 2.9 copy.22
  245.0 3.1 fusion.1
  248.2 131.5 %all-reduce.1 = f32[2,128,16]{2,1,0:T(8,128)S(1)} all-reduce(f32[2,128,16]{2,1,0:T(8,128)S(1)} %copy.23), channel_id=3, replica_groups=mesh['blk'=32,'segment'=4] {'blk'}, use_global_device_ids=true, to_apply=%region_5.6.clone | all-reduce | flops 4096 | bytes 32768
  379.8 153.2 %all-reduce.22.cloned.1.call-done = f32[2,128,2048]{2,1,0:T(8,128)} async-done(((f32[2,128,2048]{2,1,0:T(8,128)}), f32[2,128,2048]{2,1,0:T(8,128)}) %all-reduce.22.cloned.1.call-update) | async-done | bytes 2097168
  533.0 1.5 constant_dynamic-slice_fusion.1
  534.6 29.4 %psum.50 = f32[2,4,16]{2,1,0:T(4,128)S(1)} all-reduce(f32[2,4,16]{2,1,0:T(4,128)S(1)} %constant_dynamic-slice_fusion), channel_id=1, replica_groups=mesh['blk'=32,'segment'=4] {'segment'}, use_global_device_ids=true, to_apply=%region_6.7 | all-reduce | flops 128 | bytes 1024 | tf_op jit(solution)/shard_map/psum | solution.py:93
  564.2 34.6 %all-reduce.10.cloned.1.call-done = f32[2,4,2048]{2,1,0:T(4,128)} async-done(((f32[2,4,2048]{2,1,0:T(4,128)}), f32[2,4,2048]{2,1,0:T(4,128)}) %all-reduce.10.cloned.1.call-update) | async-done | bytes 65552 | tf_op jit(solution)/shard_map/psum | solution.py:93
  600.4 128.9 %all-gather.5.cloned.1.call-done = f32[2,128,2048]{2,0,1:T(2,128)} async-done(((f32[2,4,2048]{2,0,1:T(2,128)}), f32[2,128,2048]{2,0,1:T(2,128)}) %all-gather.5.cloned.1.call-update) | async-done | bytes 2097168 | tf_op jit(solution)/shard_map/all_gather | solution.py:102
  729.2 5.4 fusion.100
  737.8 2.3 collective-permute-done
  740.2 1.5 fusion.14
  741.7 311.0 %all-reduce.12.cloned.1.call-done = f32[128,2048]{1,0:T(8,128)} async-done(((f32[128,2048]{1,0:T(8,128)}), f32[128,2048]{1,0:T(8,128)}) %all-reduce.12.cloned.1.call-update) | async-done | bytes 1048592 | tf_op jit(solution)/shard_map/psum | solution.py:54
  1052.8 2.0 bitcast_add_fusion
  1054.8 28.3 %collective-permute-start.1 = (f32[128,2048]{1,0:T(8,128)S(1)}, f32[128,2048]{1,0:T(8,128)S(1)}, u32[]{:S(2)}, u32[]{:S(2)}) collective-permute-start(f32[128,2048]{1,0:T(8,128)S(1)} %bitcast_add_fusion), channel_id=1, source_target_pairs={{0,1},{1,2},{2,3},{4,5},{5,6},{6,7},{8,9},{9,10},{10,11},{12,13},{... | collective-permute-start | bytes 3145736 | tf_op jit(solution)/shard_map/ppermute | solution.py:18
  1083.1 12.2 collective-permute-done.1
  1095.4 1.9 multiply_reduce_fusion.3
  1099.4 2.8 collective-permute-done.2
  1102.2 1.5 fusion.16
  1103.7 289.7 %all-reduce.14.cloned.1.call-done = f32[128,2048]{1,0:T(8,128)} async-done(((f32[128,2048]{1,0:T(8,128)}), f32[128,2048]{1,0:T(8,128)}) %all-reduce.14.cloned.1.call-update) | async-done | bytes 1048592 | tf_op jit(solution)/shard_map/psum | solution.py:54
  1393.4 1.7 add.118
  1395.1 28.1 %collective-permute-start.3 = (f32[128,2048]{1,0:T(8,128)S(1)}, f32[128,2048]{1,0:T(8,128)S(1)}, u32[]{:S(2)}, u32[]{:S(2)}) collective-permute-start(f32[128,2048]{1,0:T(8,128)S(1)} %add.118), channel_id=1, source_target_pairs={{0,1},{1,2},{2,3},{4,5},{5,6},{6,7},{8,9},{9,10},{10,11},{12,13},{... | collective-permute-start | bytes 3145736 | tf_op jit(solution)/shard_map/ppermute | solution.py:18
  1423.2 12.4 collective-permute-done.3
  1437.7 2.8 collective-permute-done.4
  1440.6 1.5 fusion.18
  1442.1 289.7 %all-reduce.16.cloned.1.call-done = f32[128,2048]{1,0:T(8,128)} async-done(((f32[128,2048]{1,0:T(8,128)}), f32[128,2048]{1,0:T(8,128)}) %all-reduce.16.cloned.1.call-update) | async-done | bytes 1048592 | tf_op jit(solution)/shard_map/psum | solution.py:54
  1731.8 1.7 add.121
  1733.5 28.1 %collective-permute-start.5 = (f32[128,2048]{1,0:T(8,128)S(1)}, f32[128,2048]{1,0:T(8,128)S(1)}, u32[]{:S(2)}, u32[]{:S(2)}) collective-permute-start(f32[128,2048]{1,0:T(8,128)S(1)} %add.121), channel_id=1, source_target_pairs={{0,1},{1,2},{2,3},{4,5},{5,6},{6,7},{8,9},{9,10},{10,11},{12,13},{... | collective-permute-start | bytes 3145736 | tf_op jit(solution)/shard_map/ppermute | solution.py:18
  1761.6 12.4 collective-permute-done.5
  1776.2 2.8 collective-permute-done.6
  1779.0 1.5 fusion.20
  1780.6 289.6 %all-reduce.18.cloned.1.call-done = f32[128,2048]{1,0:T(8,128)} async-done(((f32[128,2048]{1,0:T(8,128)}), f32[128,2048]{1,0:T(8,128)}) %all-reduce.18.cloned.1.call-update) | async-done | bytes 1048592 | tf_op jit(solution)/shard_map/psum | solution.py:54
  2070.2 2.7 select_bitcast_fusion.1
  2072.9 28.1 %collective-permute-start.7 = (f32[128,2048]{1,0:T(8,128)S(1)}, f32[128,2048]{1,0:T(8,128)S(1)}, u32[]{:S(2)}, u32[]{:S(2)}) collective-permute-start(f32[128,2048]{1,0:T(8,128)S(1)} %get-tuple-element.6), channel_id=1, source_target_pairs={{0,1},{1,2},{2,3},{4,5},{5,6},{6,7},{8,9},{9,10},{10,11},{12,13},{... | collective-permute-start | bytes 3145736 | tf_op jit(solution)/shard_map/ppermute | solution.py:18
  2101.0 12.4 collective-permute-done.7
  2115.1 2.8 collective-permute-done.8
  2117.9 1.5 fusion.22
  2119.5 289.7 %all-reduce.20.cloned.1.call-done = f32[128,2048]{1,0:T(8,128)} async-done(((f32[128,2048]{1,0:T(8,128)}), f32[128,2048]{1,0:T(8,128)}) %all-reduce.20.cloned.1.call-update) | async-done | bytes 1048592 | tf_op jit(solution)/shard_map/psum | solution.py:54
  2409.2 1.7 select_bitcast_fusion
  2411.7 2.3 copy.33
  2414.0 3.3 reshape.239
  2417.4 55.1 %reduce-scatter.6.cloned.1.call-done = f32[512,8]{1,0:T(8,128)} async-done(((f32[2048,8]{1,0:T(8,128)}), f32[512,8]{1,0:T(8,128)}) %reduce-scatter.6.cloned.1.call-update) | async-done | bytes 16400
  (90 shorter events, 17.5 us)
Async XLA Ops:
  6.5 137.1 %copy-start = (bf16[2,256,2048]{2,1,0:T(8,128)(2,1)S(1)}, bf16[2,256,2048]{2,1,0:T(8,128)(2,1)}, u32[]{:S(2)}) copy-start(bf16[2,256,2048]{2,1,0:T(8,128)(2,1)} %param.10) | copy-start | bytes 6291460
  6.5 5.6 copy-start.10
  6.5 133.4 %all-gather.3.cloned.1.call-start = ((), (), s32[]{:S(2)}) async-start(), calls=%async_computation.1 | async-start | bytes 1081344 | tf_op jit(solution)/shard_map/all_gather | solution.py:67
  8.1 524.9 %all-reduce.22.cloned.1.call-start = ((), (), s32[]{:S(2)}) async-start(), calls=%async_computation.10 | async-start | bytes 4194304
  240.7 3.0 copy-start.11
  243.6 355.1 %copy-start.9 = (bf16[2,4,2048]{2,1,0:T(4,128)(2,1)S(1)}, bf16[2,4,2048]{2,1,0:T(4,128)(2,1)}, u32[]{:S(2)}) copy-start(bf16[2,4,2048]{2,1,0:T(4,128)(2,1)} %param.9) | copy-start | bytes 98308
  243.7 355.1 %all-reduce.10.cloned.1.call-start = ((), (), s32[]{:S(2)}) async-start(), calls=%async_computation.2 | async-start | bytes 131072 | tf_op jit(solution)/shard_map/psum | solution.py:93
  248.1 487.5 %copy-start.1 = (bf16[1,2048,3,64]{1,3,2,0:T(8,128)(2,1)S(1)}, bf16[1,2048,3,64]{1,3,2,0:T(8,128)(2,1)}, u32[]{:S(2)}) copy-start(bf16[1,2048,3,64]{1,3,2,0:T(8,128)(2,1)} %param.14) | copy-start | bytes 2359300
  248.1 487.5 %copy-start.8 = (f32[1,2048]{1,0:T(1,128)S(1)}, f32[1,2048]{1,0:T(1,128)}, u32[]{:S(2)}) copy-start(f32[1,2048]{1,0:T(1,128)} %param.13) | copy-start | bytes 24580
  534.6 205.6 %copy-start.7 = (bf16[1,64,2048]{2,1,0:T(8,128)(2,1)S(1)}, bf16[1,64,2048]{2,1,0:T(8,128)(2,1)}, u32[]{:S(2)}) copy-start(bf16[1,64,2048]{2,1,0:T(8,128)(2,1)} %param.15) | copy-start | bytes 786436
  534.6 194.7 %all-gather.5.cloned.1.call-start = ((), (), s32[]{:S(2)}) async-start(), calls=%async_computation.3 | async-start | bytes 2162688 | tf_op jit(solution)/shard_map/all_gather | solution.py:102
  600.3 452.5 %all-reduce.12.cloned.1.call-start = ((), (), s32[]{:S(2)}) async-start(), calls=%async_computation.4 | async-start | bytes 2097152 | tf_op jit(solution)/shard_map/psum | solution.py:54
  734.6 1.0 copy-start.6
  736.4 3.7 collective-permute-start
  741.7 651.7 %all-reduce.14.cloned.1.call-start = ((), (), s32[]{:S(2)}) async-start(), calls=%async_computation.5 | async-start | bytes 2097152 | tf_op jit(solution)/shard_map/psum | solution.py:54
  1054.8 40.6 %collective-permute-start.1 = (f32[128,2048]{1,0:T(8,128)S(1)}, f32[128,2048]{1,0:T(8,128)S(1)}, u32[]{:S(2)}, u32[]{:S(2)}) collective-permute-start(f32[128,2048]{1,0:T(8,128)S(1)} %bitcast_add_fusion), channel_id=1, source_target_pairs={{0,1},{1,2},{2,3},{4,5},{5,6},{6,7},{8,9},{9,10},{10,11},{12,13},{... | collective-permute-start | bytes 3145736 | tf_op jit(solution)/shard_map/ppermute | solution.py:18
  1097.2 1.0 copy-start.4
  1098.9 3.2 collective-permute-start.2
  1103.7 628.1 %all-reduce.16.cloned.1.call-start = ((), (), s32[]{:S(2)}) async-start(), calls=%async_computation.6 | async-start | bytes 2097152 | tf_op jit(solution)/shard_map/psum | solution.py:54
  1395.1 40.6 %collective-permute-start.3 = (f32[128,2048]{1,0:T(8,128)S(1)}, f32[128,2048]{1,0:T(8,128)S(1)}, u32[]{:S(2)}, u32[]{:S(2)}) collective-permute-start(f32[128,2048]{1,0:T(8,128)S(1)} %add.118), channel_id=1, source_target_pairs={{0,1},{1,2},{2,3},{4,5},{5,6},{6,7},{8,9},{9,10},{10,11},{12,13},{... | collective-permute-start | bytes 3145736 | tf_op jit(solution)/shard_map/ppermute | solution.py:18
  1435.6 1.0 copy-start.3
  1437.3 3.2 collective-permute-start.4
  1442.1 628.1 %all-reduce.18.cloned.1.call-start = ((), (), s32[]{:S(2)}) async-start(), calls=%async_computation.7 | async-start | bytes 2097152 | tf_op jit(solution)/shard_map/psum | solution.py:54
  1733.5 40.6 %collective-permute-start.5 = (f32[128,2048]{1,0:T(8,128)S(1)}, f32[128,2048]{1,0:T(8,128)S(1)}, u32[]{:S(2)}, u32[]{:S(2)}) collective-permute-start(f32[128,2048]{1,0:T(8,128)S(1)} %add.121), channel_id=1, source_target_pairs={{0,1},{1,2},{2,3},{4,5},{5,6},{6,7},{8,9},{9,10},{10,11},{12,13},{... | collective-permute-start | bytes 3145736 | tf_op jit(solution)/shard_map/ppermute | solution.py:18
  1774.0 1.0 copy-start.2
  1775.7 3.2 collective-permute-start.6
  1780.5 628.7 %all-reduce.20.cloned.1.call-start = ((), (), s32[]{:S(2)}) async-start(), calls=%async_computation.8 | async-start | bytes 2097152 | tf_op jit(solution)/shard_map/psum | solution.py:54
  2072.9 40.5 %collective-permute-start.7 = (f32[128,2048]{1,0:T(8,128)S(1)}, f32[128,2048]{1,0:T(8,128)S(1)}, u32[]{:S(2)}, u32[]{:S(2)}) collective-permute-start(f32[128,2048]{1,0:T(8,128)S(1)} %get-tuple-element.6), channel_id=1, source_target_pairs={{0,1},{1,2},{2,3},{4,5},{5,6},{6,7},{8,9},{9,10},{10,11},{12,13},{... | collective-permute-start | bytes 3145736 | tf_op jit(solution)/shard_map/ppermute | solution.py:18
  2113.4 1.0 copy-start.5
  2114.7 3.2 collective-permute-start.8
  2119.4 353.1 %reduce-scatter.6.cloned.1.call-start = ((), (), s32[]{:S(2)}) async-start(), calls=%async_computation.9 | async-start | bytes 1310720
Sparse Core Ops, SparseCore 0:
  9.0 130.9 all-gather.2
  243.8 289.1 all-reduce.21
  535.5 63.2 all-reduce.9
  600.4 128.7 all-gather.4
  741.8 310.9 all-reduce.11
  1103.8 289.5 all-reduce.13
  1442.2 289.5 all-reduce.15
  1780.6 289.4 all-reduce.17
  2119.5 289.6 all-reduce.19
  2417.5 54.9 reduce-scatter.5
where the time goes:
time: 2480 us
  waiting for transfers between devices  2030 us (82%)
  blocking collectives  248 us (10%)
  starting transfers between devices  116 us (5%)
  local copies, waits for them, and re-layouts  31.8 us (1%)
    psum x5, waiting for transfers between devices, layer_full(): return latent_state + lax.psum(update, 'blk')  1470 us
    unnamed x12, waiting for transfers between devices  208 us
    unnamed x1, blocking collectives  132 us
    all_gather x1, waiting for transfers between devices, on_device(): tower_in = lax.all_gather(start_state, 'blk', axis=1, tiled=True)  129 us
    all_gather x1, waiting for transfers between devices, on_device(): gathered = lax.all_gather(latent_queries, 'blk', axis=1, tiled=True)  128 us
    ppermute x4, starting transfers between devices, shifted(): lax.ppermute(value, axis, [(source, source + steps) for source in range(f...  113 us
    pmax x1, blocking collectives, on_device(): highest = lax.pmax(jnp.max(scores, axis=3), ('blk', 'segment'))  87.3 us
  transfers between devices with their start and end apart: 19, of which 19 were waited for; matrix products, arithmetic and copies ran while one was open for 0% of the time, Pallas kernels for 0%

commit v1 on v0

--- a/solution.py
+++ b/solution.py
@@ -64,7 +64,10 @@
     hist_rows = history_keys.shape[1]
     width = history_keys.shape[2]
     head_size = width // HEADS
-    gathered = lax.all_gather(latent_queries, "blk", axis=1, tiled=True)
+    size = lax.axis_size("blk")
+    blocks = jnp.stack([latent_queries for _ in range(size)])
+    blocks = lax.all_to_all(blocks, "blk", split_axis=0, concat_axis=0)
+    gathered = jnp.concatenate(blocks, axis=1)
     lat_count = gathered.shape[1]
     first_key = (blk_id * segment_count + segment_id) * hist_rows
     key_ids = first_key + jnp.arange(hist_rows, dtype=jnp.int32)

time: 2480 us -> 2360 us (0.952)
  waiting for transfers between devices: 2030 us -> 1920 us
    all_gather x1 -> x0, waiting for transfers between devices: 128 us -> none  [on_device(): gathered = lax.all_gather(latent_queries, 'blk', axis=1, tiled=True)]
    unnamed x12 -> x11, waiting for transfers between devices: 208 us -> 210 us
where the time goes in v1:
time: 2360 us; the launch traced here: 2350 us
  waiting for transfers between devices  1920 us (81%)
  blocking collectives  224 us (9%)
  starting transfers between devices  125 us (5%)
  local copies, waits for them, and re-layouts  34.4 us (1%)
    psum x5, waiting for transfers between devices, layer_full(): return latent_state + lax.psum(update, 'blk')  1470 us
    unnamed x11, waiting for transfers between devices  210 us
    unnamed x1, blocking collectives  130 us
    all_gather x1, waiting for transfers between devices, on_device(): tower_in = lax.all_gather(start_state, 'blk', axis=1, tiled=True)  129 us
    ppermute x4, starting transfers between devices, shifted(): lax.ppermute(value, axis, [(source, source + steps) for source in range(f...  112 us
    pmax x1, blocking collectives, on_device(): highest = lax.pmax(jnp.max(scores, axis=3), ('blk', 'segment'))  64.7 us
    ppermute x4, waiting for transfers between devices, shifted(): lax.ppermute(value, axis, [(source, source + steps) for source in range(f...  49.5 us
  transfers between devices with their start and end apart: 19, of which 19 were waited for; matrix products, arithmetic and copies ran while one was open for 0% of the time, Pallas kernels for 0%

profile of v1, /device:TPU:1, one launch (start us, length us, event | category | flops | bytes accessed | tf_op | source)
XLA Modules:
  0.0 2354.2 jit_solution(15061850140836011860)
XLA Ops:
  6.5 2.5 stack.8
  9.0 9.3 all-to-all-start
  18.4 4.0 copy.25
  22.5 12.1 all-to-all-done
  34.6 2.8 copy.16
  37.4 2.5 reshape_reshape.3
  39.9 4.2 fusion
  44.1 64.7 %pmax.7 = f32[2,16,128]{2,1,0:T(8,128)S(1)} all-reduce(f32[2,16,128]{2,1,0:T(8,128)S(1)} %get-tuple-element.11), channel_id=1, replica_groups=mesh['blk'=32,'segment'=4] {'blk','segment'}, use_global_device_ids=true, to_apply=%region_1.2 | all-reduce | flops 4096 | bytes 32768 | tf_op jit(solution)/shard_map/pmax | solution.py:82
  108.8 5.4 fusion.3
  114.2 2.9 copy.20
  118.4 3.1 fusion.1
  121.7 130.4 %all-reduce.1 = f32[2,128,16]{2,1,0:T(8,128)S(1)} all-reduce(f32[2,128,16]{2,1,0:T(8,128)S(1)} %copy.21), channel_id=3, replica_groups=mesh['blk'=32,'segment'=4] {'blk'}, use_global_device_ids=true, to_apply=%region_5.6.clone | all-reduce | flops 4096 | bytes 32768
  252.1 154.3 %all-reduce.22.cloned.1.call-done = f32[2,128,2048]{2,1,0:T(8,128)} async-done(((f32[2,128,2048]{2,1,0:T(8,128)}), f32[2,128,2048]{2,1,0:T(8,128)}) %all-reduce.22.cloned.1.call-update) | async-done | bytes 2097168
  406.4 1.5 constant_dynamic-slice_fusion.1
  408.0 29.4 %psum.50 = f32[2,4,16]{2,1,0:T(4,128)S(1)} all-reduce(f32[2,4,16]{2,1,0:T(4,128)S(1)} %constant_dynamic-slice_fusion), channel_id=1, replica_groups=mesh['blk'=32,'segment'=4] {'segment'}, use_global_device_ids=true, to_apply=%region_6.7 | all-reduce | flops 128 | bytes 1024 | tf_op jit(solution)/shard_map/psum | solution.py:96
  437.6 34.6 %all-reduce.10.cloned.1.call-done = f32[2,4,2048]{2,1,0:T(4,128)} async-done(((f32[2,4,2048]{2,1,0:T(4,128)}), f32[2,4,2048]{2,1,0:T(4,128)}) %all-reduce.10.cloned.1.call-update) | async-done | bytes 65552 | tf_op jit(solution)/shard_map/psum | solution.py:96
  473.8 128.9 %all-gather.2.cloned.1.call-done = f32[2,128,2048]{2,0,1:T(2,128)} async-done(((f32[2,4,2048]{2,0,1:T(2,128)}), f32[2,128,2048]{2,0,1:T(2,128)}) %all-gather.2.cloned.1.call-update) | async-done | bytes 2097168 | tf_op jit(solution)/shard_map/all_gather | solution.py:105
  602.7 5.4 fusion.101
  611.2 2.6 collective-permute-done
  615.5 310.4 %all-reduce.12.cloned.1.call-done = f32[128,2048]{1,0:T(8,128)} async-done(((f32[128,2048]{1,0:T(8,128)}), f32[128,2048]{1,0:T(8,128)}) %all-reduce.12.cloned.1.call-update) | async-done | bytes 1048592 | tf_op jit(solution)/shard_map/psum | solution.py:54
  925.9 2.0 bitcast_add_fusion
  927.9 28.3 %collective-permute-start.1 = (f32[128,2048]{1,0:T(8,128)S(1)}, f32[128,2048]{1,0:T(8,128)S(1)}, u32[]{:S(2)}, u32[]{:S(2)}) collective-permute-start(f32[128,2048]{1,0:T(8,128)S(1)} %bitcast_add_fusion), channel_id=1, source_target_pairs={{0,1},{1,2},{2,3},{4,5},{5,6},{6,7},{8,9},{9,10},{10,11},{12,13},{... | collective-permute-start | bytes 3145736 | tf_op jit(solution)/shard_map/ppermute | solution.py:18
  956.3 12.2 collective-permute-done.1
  968.5 1.9 multiply_reduce_fusion.3
  972.5 2.8 collective-permute-done.2
  975.3 1.5 fusion.16
  976.8 289.7 %all-reduce.14.cloned.1.call-done = f32[128,2048]{1,0:T(8,128)} async-done(((f32[128,2048]{1,0:T(8,128)}), f32[128,2048]{1,0:T(8,128)}) %all-reduce.14.cloned.1.call-update) | async-done | bytes 1048592 | tf_op jit(solution)/shard_map/psum | solution.py:54
  1266.6 1.7 add.118
  1268.2 28.1 %collective-permute-start.3 = (f32[128,2048]{1,0:T(8,128)S(1)}, f32[128,2048]{1,0:T(8,128)S(1)}, u32[]{:S(2)}, u32[]{:S(2)}) collective-permute-start(f32[128,2048]{1,0:T(8,128)S(1)} %add.118), channel_id=1, source_target_pairs={{0,1},{1,2},{2,3},{4,5},{5,6},{6,7},{8,9},{9,10},{10,11},{12,13},{... | collective-permute-start | bytes 3145736 | tf_op jit(solution)/shard_map/ppermute | solution.py:18
  1296.4 12.4 collective-permute-done.3
  1310.9 2.8 collective-permute-done.4
  1313.7 1.5 fusion.18
  1315.3 289.6 %all-reduce.16.cloned.1.call-done = f32[128,2048]{1,0:T(8,128)} async-done(((f32[128,2048]{1,0:T(8,128)}), f32[128,2048]{1,0:T(8,128)}) %all-reduce.16.cloned.1.call-update) | async-done | bytes 1048592 | tf_op jit(solution)/shard_map/psum | solution.py:54
  1604.8 1.7 add.121
  1606.5 28.1 %collective-permute-start.5 = (f32[128,2048]{1,0:T(8,128)S(1)}, f32[128,2048]{1,0:T(8,128)S(1)}, u32[]{:S(2)}, u32[]{:S(2)}) collective-permute-start(f32[128,2048]{1,0:T(8,128)S(1)} %add.121), channel_id=1, source_target_pairs={{0,1},{1,2},{2,3},{4,5},{5,6},{6,7},{8,9},{9,10},{10,11},{12,13},{... | collective-permute-start | bytes 3145736 | tf_op jit(solution)/shard_map/ppermute | solution.py:18
  1634.6 12.4 collective-permute-done.5
  1649.2 2.8 collective-permute-done.6
  1652.0 1.5 fusion.20
  1653.6 290.3 %all-reduce.18.cloned.1.call-done = f32[128,2048]{1,0:T(8,128)} async-done(((f32[128,2048]{1,0:T(8,128)}), f32[128,2048]{1,0:T(8,128)}) %all-reduce.18.cloned.1.call-update) | async-done | bytes 1048592 | tf_op jit(solution)/shard_map/psum | solution.py:54
  1943.8 2.7 select_bitcast_fusion.1
  1946.6 27.4 %collective-permute-start.7 = (f32[128,2048]{1,0:T(8,128)S(1)}, f32[128,2048]{1,0:T(8,128)S(1)}, u32[]{:S(2)}, u32[]{:S(2)}) collective-permute-start(f32[128,2048]{1,0:T(8,128)S(1)} %get-tuple-element.6), channel_id=1, source_target_pairs={{0,1},{1,2},{2,3},{4,5},{5,6},{6,7},{8,9},{9,10},{10,11},{12,13},{... | collective-permute-start | bytes 3145736 | tf_op jit(solution)/shard_map/ppermute | solution.py:18
  1974.0 12.4 collective-permute-done.7
  1988.0 2.8 collective-permute-done.8
  1992.5 289.9 %all-reduce.20.cloned.1.call-done = f32[128,2048]{1,0:T(8,128)} async-done(((f32[128,2048]{1,0:T(8,128)}), f32[128,2048]{1,0:T(8,128)}) %all-reduce.20.cloned.1.call-update) | async-done | bytes 1048592 | tf_op jit(solution)/shard_map/psum | solution.py:54
  2282.4 1.7 select_bitcast_fusion
  2284.9 2.3 copy.30
  2287.2 3.3 reshape.241
  2290.6 55.0 %reduce-scatter.6.cloned.1.call-done = f32[512,8]{1,0:T(8,128)} async-done(((f32[2048,8]{1,0:T(8,128)}), f32[512,8]{1,0:T(8,128)}) %reduce-scatter.6.cloned.1.call-update) | async-done | bytes 16400
  (90 shorter events, 20.3 us)
Async XLA Ops:
  6.5 33.4 %copy-start = (bf16[2,256,2048]{2,1,0:T(8,128)(2,1)S(1)}, bf16[2,256,2048]{2,1,0:T(8,128)(2,1)}, u32[]{:S(2)}) copy-start(bf16[2,256,2048]{2,1,0:T(8,128)(2,1)} %param.10) | copy-start | bytes 6291460
  6.5 15.8 copy-start.10
  9.0 25.6 %all-to-all-start = ((bf16[32,2,4,2048]{3,2,1,0:T(4,128)(2,1)}), bf16[32,2,4,2048]{3,2,1,0:T(4,128)(2,1)}, u32[]{:S(2)}, u32[]{:S(2)}) async-start(bf16[32,2,4,2048]{3,2,1,0:T(4,128)(2,1)} %stack.8), calls=%async_computation | async-start | bytes 2097152 | tf_op jit(solution)/shard_map/all_to_all | solution.py:69
  18.4 388.0 %all-reduce.22.cloned.1.call-start = ((), (), s32[]{:S(2)}) async-start(), calls=%async_computation.10 | async-start | bytes 4194304
  114.2 3.0 copy-start.11
  117.1 355.1 %copy-start.9 = (bf16[2,4,2048]{2,1,0:T(4,128)(2,1)S(1)}, bf16[2,4,2048]{2,1,0:T(4,128)(2,1)}, u32[]{:S(2)}) copy-start(bf16[2,4,2048]{2,1,0:T(4,128)(2,1)} %param.9) | copy-start | bytes 98308
  117.1 355.0 %all-reduce.10.cloned.1.call-start = ((), (), s32[]{:S(2)}) async-start(), calls=%async_computation.2 | async-start | bytes 131072 | tf_op jit(solution)/shard_map/psum | solution.py:96
  121.5 487.5 %copy-start.1 = (bf16[1,2048,3,64]{1,3,2,0:T(8,128)(2,1)S(1)}, bf16[1,2048,3,64]{1,3,2,0:T(8,128)(2,1)}, u32[]{:S(2)}) copy-start(bf16[1,2048,3,64]{1,3,2,0:T(8,128)(2,1)} %param.14) | copy-start | bytes 2359300
  121.6 487.5 %copy-start.8 = (f32[1,2048]{1,0:T(1,128)S(1)}, f32[1,2048]{1,0:T(1,128)}, u32[]{:S(2)}) copy-start(f32[1,2048]{1,0:T(1,128)} %param.13) | copy-start | bytes 24580
  408.0 206.0 %copy-start.7 = (bf16[1,64,2048]{2,1,0:T(8,128)(2,1)S(1)}, bf16[1,64,2048]{2,1,0:T(8,128)(2,1)}, u32[]{:S(2)}) copy-start(bf16[1,64,2048]{2,1,0:T(8,128)(2,1)} %param.15) | copy-start | bytes 786436
  408.0 194.7 %all-gather.2.cloned.1.call-start = ((), (), s32[]{:S(2)}) async-start(), calls=%async_computation.3 | async-start | bytes 2162688 | tf_op jit(solution)/shard_map/all_gather | solution.py:105
  473.7 452.2 %all-reduce.12.cloned.1.call-start = ((), (), s32[]{:S(2)}) async-start(), calls=%async_computation.4 | async-start | bytes 2097152 | tf_op jit(solution)/shard_map/psum | solution.py:54
  608.1 1.0 copy-start.6
  609.9 3.9 collective-permute-start
  615.4 651.1 %all-reduce.14.cloned.1.call-start = ((), (), s32[]{:S(2)}) async-start(), calls=%async_computation.5 | async-start | bytes 2097152 | tf_op jit(solution)/shard_map/psum | solution.py:54
  927.9 40.6 %collective-permute-start.1 = (f32[128,2048]{1,0:T(8,128)S(1)}, f32[128,2048]{1,0:T(8,128)S(1)}, u32[]{:S(2)}, u32[]{:S(2)}) collective-permute-start(f32[128,2048]{1,0:T(8,128)S(1)} %bitcast_add_fusion), channel_id=1, source_target_pairs={{0,1},{1,2},{2,3},{4,5},{5,6},{6,7},{8,9},{9,10},{10,11},{12,13},{... | collective-permute-start | bytes 3145736 | tf_op jit(solution)/shard_map/ppermute | solution.py:18
  970.4 1.0 copy-start.4
  972.0 3.2 collective-permute-start.2
  976.8 628.0 %all-reduce.16.cloned.1.call-start = ((), (), s32[]{:S(2)}) async-start(), calls=%async_computation.6 | async-start | bytes 2097152 | tf_op jit(solution)/shard_map/psum | solution.py:54
  1268.2 40.6 %collective-permute-start.3 = (f32[128,2048]{1,0:T(8,128)S(1)}, f32[128,2048]{1,0:T(8,128)S(1)}, u32[]{:S(2)}, u32[]{:S(2)}) collective-permute-start(f32[128,2048]{1,0:T(8,128)S(1)} %add.118), channel_id=1, source_target_pairs={{0,1},{1,2},{2,3},{4,5},{5,6},{6,7},{8,9},{9,10},{10,11},{12,13},{... | collective-permute-start | bytes 3145736 | tf_op jit(solution)/shard_map/ppermute | solution.py:18
  1308.8 1.0 copy-start.3
  1310.4 3.2 collective-permute-start.4
  1315.2 628.6 %all-reduce.18.cloned.1.call-start = ((), (), s32[]{:S(2)}) async-start(), calls=%async_computation.7 | async-start | bytes 2097152 | tf_op jit(solution)/shard_map/psum | solution.py:54
  1606.5 40.6 %collective-permute-start.5 = (f32[128,2048]{1,0:T(8,128)S(1)}, f32[128,2048]{1,0:T(8,128)S(1)}, u32[]{:S(2)}, u32[]{:S(2)}) collective-permute-start(f32[128,2048]{1,0:T(8,128)S(1)} %add.121), channel_id=1, source_target_pairs={{0,1},{1,2},{2,3},{4,5},{5,6},{6,7},{8,9},{9,10},{10,11},{12,13},{... | collective-permute-start | bytes 3145736 | tf_op jit(solution)/shard_map/ppermute | solution.py:18
  1647.0 1.0 copy-start.2
  1648.7 3.2 collective-permute-start.6
  1653.5 628.9 %all-reduce.20.cloned.1.call-start = ((), (), s32[]{:S(2)}) async-start(), calls=%async_computation.8 | async-start | bytes 2097152 | tf_op jit(solution)/shard_map/psum | solution.py:54
  1946.6 39.8 %collective-permute-start.7 = (f32[128,2048]{1,0:T(8,128)S(1)}, f32[128,2048]{1,0:T(8,128)S(1)}, u32[]{:S(2)}, u32[]{:S(2)}) collective-permute-start(f32[128,2048]{1,0:T(8,128)S(1)} %get-tuple-element.6), channel_id=1, source_target_pairs={{0,1},{1,2},{2,3},{4,5},{5,6},{6,7},{8,9},{9,10},{10,11},{12,13},{... | collective-permute-start | bytes 3145736 | tf_op jit(solution)/shard_map/ppermute | solution.py:18
  1986.4 1.0 copy-start.5
  1987.6 3.2 collective-permute-start.8
  1992.4 353.2 %reduce-scatter.6.cloned.1.call-start = ((), (), s32[]{:S(2)}) async-start(), calls=%async_computation.9 | async-start | bytes 1310720
Sparse Core Ops, SparseCore 0:
  117.2 289.1 all-reduce.21
  408.9 63.2 all-reduce.9
  473.8 128.8 all-gather.1
  615.5 310.3 all-reduce.11
  976.9 289.5 all-reduce.13
  1315.3 289.4 all-reduce.15
  1653.6 290.1 all-reduce.17
  1992.5 289.7 all-reduce.19
  2290.7 54.8 reduce-scatter.5
